TPU v7x, 128 devices: a whole 4x4x4 slice. The times are simulated.
128 devices in a mesh: ctx: 64 (over y_lo, x, z, core), tp: 2 (over y_hi).
Axes of the slice: x: 4, y: 4 (y_hi: 2, y_lo: 2; y = y_hi * 2 + y_lo), z: 4, core: 2. Of those that a mesh axis runs over, the one named last changes fastest.
Arguments:
- inputs: bfloat16 [3, 8192, 4096], P(None, 'ctx', 'tp'), may hold values from -6 to 6
- short_weight: float32 [3, 3, 4096], P(None, None, 'tp'), may hold values from -3 to 3
- taps: float32 [8192, 4096], P('ctx', 'tp'), may hold values from -6 to 6
- w_out: bfloat16 [4096, 4096], P('tp'), may hold values from -0.09375 to 0.09375
- grad_out: bfloat16 [8192, 4096], P('ctx', 'tp'), may hold values from -6 to 6
Outputs:
- inputs_grad: bfloat16 [3, 8192, 4096], P(None, 'ctx', 'tp')
- taps_grad: float32 [8192, 4096], P('ctx', 'tp')
- short_grad: float32 [3, 3, 4096], P(None, None, 'tp')
All inputs are finite; a program needn't handle non-finite values.
Results may differ from a plain program's by a relative error of at most 0.0015.
Values may be sent and summed in bfloat16 or wider, within the bound.
No kernel may reach another device: no remote copies, remote signals or barrier semaphores. Data moves between devices by JAX's collectives and lax.ppermute only.
A program may use at most 192 MiB of HBM per device.

v0:
```python
import math
import jax
import jax.numpy as jnp
from jax import lax
from jax.sharding import PartitionSpec as P

HIGH = lax.Precision.HIGHEST


def shifted(x, axis, by):
    peers = lax.axis_size(axis)
    pairs = [(i, i + by) for i in range(peers) if 0 <= i + by < peers]
    return lax.ppermute(x, axis, pairs)


def phase(left_idx, right_idx, period):
    turns = left_idx[:, None] * right_idx[None, :] % period
    angle = turns.astype(jnp.float32) * (2.0 * math.pi / period)
    return (jnp.cos(angle), jnp.sin(angle))


def section_one(blocks, n2_start, period):
    count = blocks.shape[1]
    width = blocks.shape[2]
    cos_a, sin_a = phase(
        jnp.arange(2 * count, dtype=jnp.int32), jnp.arange(count, dtype=jnp.int32), 2 * count
    )
    real_part = jnp.einsum("kn,bnmc->bkmc", cos_a, blocks, precision=HIGH)
    imag_part = -jnp.einsum("kn,bnmc->bkmc", sin_a, blocks, precision=HIGH)
    cos_b, sin_b = phase(
        jnp.arange(2 * count, dtype=jnp.int32),
        n2_start + jnp.arange(width, dtype=jnp.int32),
        period,
    )
    tw_re = cos_b[None, :, :, None]
    tw_im = -sin_b[None, :, :, None]
    return jnp.stack([real_part * tw_re - imag_part * tw_im, real_part * tw_im + imag_part * tw_re])


def section_two(parts):
    length = parts.shape[3]
    cos_a, sin_a = phase(
        jnp.arange(length, dtype=jnp.int32), jnp.arange(length, dtype=jnp.int32), length
    )
    real_in, imag_in = (parts[0], parts[1])
    cc_re = jnp.einsum("qn,bknc->bkqc", cos_a, real_in, precision=HIGH)
    cc_im = jnp.einsum("qn,bknc->bkqc", cos_a, imag_in, precision=HIGH)
    ss_re = jnp.einsum("qn,bknc->bkqc", sin_a, real_in, precision=HIGH)
    ss_im = jnp.einsum("qn,bknc->bkqc", sin_a, imag_in, precision=HIGH)
    return jnp.stack([cc_re + ss_im, cc_im - ss_re])


def inverse_two(spec, k1_start, period):
    classes = spec.shape[2]
    length = spec.shape[3]
    cos_a, sin_a = phase(
        jnp.arange(length, dtype=jnp.int32), jnp.arange(length, dtype=jnp.int32), length
    )
    real_in, imag_in = (spec[0], spec[1])
    cc_re = jnp.einsum("nq,bkqc->bknc", cos_a, real_in, precision=HIGH)
    cc_im = jnp.einsum("nq,bkqc->bknc", cos_a, imag_in, precision=HIGH)
    ss_re = jnp.einsum("nq,bkqc->bknc", sin_a, real_in, precision=HIGH)
    ss_im = jnp.einsum("nq,bkqc->bknc", sin_a, imag_in, precision=HIGH)
    back_re = cc_re - ss_im
    back_im = cc_im + ss_re
    cos_b, sin_b = phase(
        k1_start + jnp.arange(classes, dtype=jnp.int32), jnp.arange(length, dtype=jnp.int32), period
    )
    tw_re = cos_b[None, :, :, None]
    tw_im = sin_b[None, :, :, None]
    return jnp.stack([back_re * tw_re - back_im * tw_im, back_re * tw_im + back_im * tw_re])


def inverse_one(spec, period):
    classes = spec.shape[2]
    count = classes // 2
    cos_a, sin_a = phase(
        jnp.arange(count, dtype=jnp.int32), jnp.arange(classes, dtype=jnp.int32), classes
    )
    real_out = jnp.einsum("nk,bkmc->bnmc", cos_a, spec[0], precision=HIGH)
    real_out = real_out - jnp.einsum("nk,bkmc->bnmc", sin_a, spec[1], precision=HIGH)
    return real_out / period


def products(spec):
    filt_re, filt_im = (spec[0, 0], spec[1, 0])
    prod_re, prod_im = (spec[0, 1], spec[1, 1])
    grad_re, grad_im = (spec[0, 2], spec[1, 2])
    out_re = jnp.stack(
        [
            filt_re * prod_re - filt_im * prod_im,
            filt_re * grad_re + filt_im * grad_im,
            prod_re * grad_re + prod_im * grad_im,
        ]
    )
    out_im = jnp.stack(
        [
            filt_re * prod_im + filt_im * prod_re,
            filt_re * grad_im - filt_im * grad_re,
            prod_re * grad_im - prod_im * grad_re,
        ]
    )
    return jnp.stack([out_re, out_im])


def shards(inputs, short_weight, taps, w_out, grad_out):
    rows = inputs.shape[1]
    span = short_weight.shape[1]
    count = lax.axis_size("ctx")
    where = lax.axis_index("ctx")
    period = 2 * count * rows
    scale = 1.0 / math.sqrt(count * rows)
    prior = shifted(inputs[:, rows - (span - 1) :, :], "ctx", 1)
    extended = jnp.concatenate([prior, inputs], axis=1).astype(jnp.float32)
    mixed = jnp.zeros((3, rows, inputs.shape[2]), jnp.float32)
    for j in range(span):
        mixed = (
            mixed + short_weight[:, j][:, None, :] * extended[:, span - 1 - j : span - 1 - j + rows]
        )
    query, key_s, value = (mixed[0], mixed[1], mixed[2])
    product = key_s * value
    filt = taps * scale
    columns = w_out
    gated_grad = lax.dot_general(
        lax.all_gather(grad_out, "tp", axis=1, tiled=True),
        columns,
        (((1,), (1,)), ((), ())),
        preferred_element_type=jnp.float32,
    )
    dy = gated_grad * query
    stacked = jnp.stack([filt, product, dy])
    width = rows // count
    blocks = stacked.reshape(3, count, width, stacked.shape[2])
    columns = section_one(
        lax.all_to_all(blocks, "ctx", split_axis=1, concat_axis=1, tiled=True),
        n2_start=where * width,
        period=period,
    )
    spec = section_two(lax.all_to_all(columns, "ctx", split_axis=2, concat_axis=3, tiled=True))
    back = inverse_two(products(spec), where * spec.shape[2], period)
    parted = inverse_one(
        lax.all_to_all(back, "ctx", split_axis=3, concat_axis=2, tiled=True), period=period
    )
    result = lax.all_to_all(parted, "ctx", split_axis=1, concat_axis=1, tiled=True).reshape(
        3, rows, stacked.shape[2]
    )
    conv_out, dz, raw = (result[0], result[1], result[2])
    dmixed = jnp.stack([gated_grad * conv_out, dz * value, dz * key_s])
    following = shifted(dmixed[:, : span - 1, :].astype(jnp.bfloat16), "ctx", -1).astype(
        jnp.float32
    )
    dext = jnp.concatenate([dmixed, following], axis=1)
    inputs_grad = jnp.zeros_like(dmixed)
    sums = []
    for j in range(span):
        inputs_grad = inputs_grad + short_weight[:, j][:, None, :] * dext[:, j : j + rows]
        sums.append(jnp.sum(dmixed * extended[:, span - 1 - j : span - 1 - j + rows], axis=1))
    short_grad = lax.psum(jnp.stack(sums, axis=1), "ctx") * scale
    return (inputs_grad.astype(jnp.bfloat16), raw * scale, short_grad)


def solution(mesh):
    return jax.shard_map(
        shards,
        mesh=mesh,
        in_specs=(
            P(None, "ctx", "tp"),
            P(None, None, "tp"),
            P("ctx", "tp"),
            P("tp", None),
            P("ctx", "tp"),
        ),
        out_specs=(P(None, "ctx", "tp"), P("ctx", "tp"), P(None, None, "tp")),
        check_vma=False,
    )
```

profile of v0, /device:TPU:0, one launch (start us, length us, event | category | flops | bytes accessed | tf_op | source)
XLA Modules:
  0.0 1261.6 jit_solution(7700438997746411273)
XLA Ops:
  17.1 3.0 stack.69
  20.1 19.3 %all-gather.2.cloned.1.call-done = bf16[128,4096]{1,0:T(8,128)(2,1)} async-done(((bf16[128,2048]{1,0:T(8,128)(2,1)}), bf16[128,4096]{1,0:T(8,128)(2,1)}) %all-gather.2.cloned.1.call-update) | async-done | bytes 1048592 | tf_op jit(solution)/shard_map/all_gather | solution.py:125
  39.4 13.1 %fusion.17 = (f32[128,2048]{1,0:T(8,128)}, f32[128,2048]{1,0:T(8,128)}) fusion(f32[3,128,2048]{2,1,0:T(8,128)S(1)} %multiply_add_fusion, bf16[128,4096]{1,0:T(8,128)(2,1)} %all-gather.2.cloned.1.call-done, bf16[2048,4096]{1,0:T(8,128)(2,1)} %param.8), kind=kOutput, calls=%fused_computation.48 | convolution fusion | flops 2147745792 | bytes 20971520 | tf_op jit(solution)/shard_map/dot_general | solution.py:124
  52.5 1.8 stack.70
  54.3 3.2 pad_maximum_fusion.13
  57.5 3.0 copy.33
  60.5 7.9 all-to-all-start
  68.5 40.4 %all-to-all-done = f32[3,64,2,2048]{3,2,0,1:T(2,128)S(1)} async-done(((f32[3,64,2,2048]{3,2,0,1:T(2,128)}), f32[3,64,2,2048]{3,2,0,1:T(2,128)S(1)}, u32[]{:S(2)}, u32[]{:S(2)}) %all-to-all-start) | async-done | bytes 3145760 | tf_op jit(solution)/shard_map/all_to_all | solution.py:135
  108.9 11.2 fusion.13
  120.1 23.9 %fusion.1 = (f32[1,3,128,2,2048]{2,4,3,1,0:T(8,128)}, f32[1,3,128,2,2048]{2,4,3,1,0:T(8,128)}) fusion(f32[3,2,2048,128]{3,2,1,0:T(8,128)S(1)} %fusion.13, f32[128,2]{0,1:T(2,128)S(1)} %get-tuple-element.38, f32[128,2]{0,1:T(2,128)S(1)} %get-tuple-element.37, f32[3,64,2,2048]{3,2,0,1:T(2,128)S(1)} %all-to-all-done), kind=kOutput, calls=%fused_computation.7 | convolution fusion | flops 1219084288 | bytes 22022144 | tf_op jit(solution)/shard_map/kn,bnmc->bkmc/dot_general | solution.py:28
  144.1 9.9 pad_maximum_fusion
  154.0 19.3 %copy.36 = f32[2,3,128,2,2048]{4,3,1,0,2:T(2,128)} copy(f32[2,3,128,2,2048]{2,4,3,1,0:T(8,128)} %pad_maximum_fusion) | data formatting | bytes 25165824 | tf_op jit(solution)/shard_map/stack | solution.py:37
  173.4 6.8 all-to-all-start.1
  180.4 160.9 %all-to-all-done.1 = f32[2,3,128,2,2048]{4,3,1,0,2:T(2,128)} async-done(((f32[2,3,128,2,2048]{4,3,1,0,2:T(2,128)}), f32[2,3,128,2,2048]{4,3,1,0,2:T(2,128)}, u32[]{:S(2)}, u32[]{:S(2)}) %all-to-all-start.1) | async-done | bytes 12582944 | tf_op jit(solution)/shard_map/all_to_all | solution.py:139
  341.3 6.3 copy.37
  347.6 3.9 fusion.131
  351.5 8.9 copy.38
  360.4 10.3 copy.39
  370.7 9.9 fusion.29
  380.7 8.8 copy.40
  389.5 10.2 copy.41
  399.7 8.1 fusion.27
  407.9 7.9 add_bitcast_fusion.1
  415.9 5.4 subtract_bitcast_fusion.1
  421.3 2.6 add_bitcast_fusion.4
  423.9 3.7 subtract_bitcast_fusion.4
  427.6 8.5 fusion.4
  436.2 5.7 fusion.5
  442.0 5.7 fusion.8
  447.6 10.8 subtract_bitcast_fusion
  458.4 8.1 pad_maximum_fusion.1
  466.5 19.3 %copy.44 = f32[2,3,2,128,2048]{4,2,1,0,3:T(2,128)} copy(f32[2,3,2,128,2048]{3,4,2,1,0:T(8,128)} %pad_maximum_fusion.1) | data formatting | bytes 25165824 | tf_op jit(solution)/shard_map/stack | solution.py:71
  485.9 166.0 %all_to_all.40 = f32[2,3,2,128,2048]{4,2,1,0,3:T(2,128)S(1)} all-to-all(f32[2,3,2,128,2048]{4,2,1,0,3:T(2,128)} %copy.44), channel_id=1, replica_groups=mesh['ctx'=64,'tp'=2] {'ctx'}, dimensions={3} | all-to-all | bytes 25165824 | tf_op jit(solution)/shard_map/all_to_all | solution.py:142
  651.9 2.8 copy.45
  654.7 3.9 fusion.130
  658.6 5.6 copy.46
  664.2 8.5 squeeze.33
  672.7 7.4 fusion.41
  680.1 5.6 copy.47
  685.7 8.6 squeeze.34
  694.4 6.5 multiply_bitcast_fusion
  700.9 2.4 copy.48
  703.3 51.2 %all_to_all.41 = f32[3,64,2,2048]{3,2,0,1:T(2,128)S(1)} all-to-all(f32[3,64,2,2048]{3,2,0,1:T(2,128)S(1)} %copy.48), channel_id=1, replica_groups=mesh['ctx'=64,'tp'=2] {'ctx'}, dimensions={1} | all-to-all | bytes 6291456 | tf_op jit(solution)/shard_map/all_to_all | solution.py:144
  754.5 2.4 slice_multiply_fusion.2
  756.9 3.1 squeeze.35
  760.0 2.9 squeeze.36
  769.2 3.0 multiply_reduce_fusion.2
  774.6 478.2 %all-reduce.2.cloned.1.call-done = f32[3,3,2048]{2,0,1:T(4,128)} async-done(((f32[3,3,2048]{2,0,1:T(4,128)}), f32[3,3,2048]{2,0,1:T(4,128)}) %all-reduce.2.cloned.1.call-update) | async-done | bytes 73744 | tf_op jit(solution)/shard_map/psum | solution.py:158
  (86 shorter events, 20.3 us)
Async XLA Ops:
  7.2 6.6 copy-start.16
  7.2 32.2 %all-gather.2.cloned.1.call-start = ((), (), s32[]{:S(2)}) async-start(), calls=%async_computation.4 | async-start | bytes 1572864 | tf_op jit(solution)/shard_map/all_gather | solution.py:125
  8.3 5.5 collective-permute-start
  12.1 2.2 copy-start.17
  12.1 2.2 copy-start.19
  12.1 2.1 copy-start.21
  14.2 1.7 copy-start
  15.9 36.6 %copy-start.4 = (f32[3,128,2048]{2,1,0:T(8,128)}, f32[3,128,2048]{2,1,0:T(8,128)S(1)}, u32[]{:S(2)}) copy-start(f32[3,128,2048]{2,1,0:T(8,128)S(1)} %multiply_add_fusion) | copy-start | bytes 9437188
  60.5 48.4 %all-to-all-start = ((f32[3,64,2,2048]{3,2,0,1:T(2,128)}), f32[3,64,2,2048]{3,2,0,1:T(2,128)S(1)}, u32[]{:S(2)}, u32[]{:S(2)}) async-start(f32[3,64,2,2048]{3,2,0,1:T(2,128)} %copy.33), calls=%async_computation | async-start | bytes 6291456 | tf_op jit(solution)/shard_map/all_to_all | solution.py:135
  173.4 167.9 %all-to-all-start.1 = ((f32[2,3,128,2,2048]{4,3,1,0,2:T(2,128)}), f32[2,3,128,2,2048]{4,3,1,0,2:T(2,128)}, u32[]{:S(2)}, u32[]{:S(2)}) async-start(f32[2,3,128,2,2048]{4,3,1,0,2:T(2,128)} %copy.36), calls=%async_computation.1 | async-start | bytes 25165824 | tf_op jit(solution)/shard_map/all_to_all | solution.py:139
  180.2 1072.5 %all-reduce.2.cloned.1.call-start = ((), (), s32[]{:S(2)}) async-start(), calls=%async_computation.5 | async-start | bytes 196608 | tf_op jit(solution)/shard_map/psum | solution.py:158
  360.4 20.3 %slice-start.2 = ((s8[6291456]{0:T(1024)(128)(4,1)}), s8[2097152]{0:T(1024)(128)(4,1)S(1)}, s32[]{:S(2)}) async-start(s8[6291456]{0:T(1024)(128)(4,1)} %bitcast.146), calls=%async_computation.8 | async-start | bytes 4194304
  370.7 10.0 slice-start.3
  399.7 8.1 copy-start.2
  399.7 16.1 %slice-start = ((s8[6291456]{0:T(1024)(128)(4,1)}), s8[4194304]{0:T(1024)(128)(4,1)S(1)}, s32[]{:S(2)}) async-start(s8[6291456]{0:T(1024)(128)(4,1)} %bitcast.140), calls=%async_computation.6 | async-start | bytes 8388608
  407.9 8.0 slice-start.1
  427.6 8.5 copy-start.9
  427.6 8.5 copy-start.10
  427.6 8.5 copy-start.11
  436.2 5.7 copy-start.6
  436.2 5.7 copy-start.7
  436.2 5.7 copy-start.8
  672.7 7.4 copy-start.3
  685.7 8.6 copy-start.12
  756.9 6.0 copy-start.5
  762.9 1.6 copy-start.13
  762.9 1.9 copy-start.14
  765.3 3.9 copy-start.1
  765.3 3.9 copy-start.18
  765.3 3.9 copy-start.20
  765.3 3.9 copy-start.22
  765.3 3.4 collective-permute-start.1
  769.2 3.7 copy-start.15
Sparse Core Ops, SparseCore 0:
  9.7 29.6 all-gather.1
  773.0 479.6 all-reduce.1
where the time goes:
time: 1270 us; the launch traced here: 1260 us
  waiting for transfers between devices  701 us (55%)
  blocking collectives  217 us (17%)
  local copies, waits for them, and re-layouts  146 us (11%)
  matrix products  124 us (10%)
  other arithmetic  41.3 us (3%)
  starting transfers between devices  17.6 us (1%)
  between operations  15 us (1%)
    psum x1, waiting for transfers between devices, shards(): short_grad = lax.psum(jnp.stack(sums, axis=1), 'ctx') * scale  478 us
    all_to_all x1, blocking collectives, shards(): lax.all_to_all(back, 'ctx', split_axis=3, concat_axis=2, tiled=True)  166 us
    all_to_all x1, waiting for transfers between devices, shards(): lax.all_to_all(columns, 'ctx', split_axis=2, concat_axis=3, tiled=True)  161 us
    all_to_all x1, blocking collectives, shards(): lax.all_to_all(parted, 'ctx', split_axis=1, concat_axis=1, tiled=True)  51.2 us
    all_to_all x1, waiting for transfers between devices, shards(): lax.all_to_all(blocks, 'ctx', split_axis=1, concat_axis=1, tiled=True)  40.4 us
  transfers between devices with their start and end apart: 6, of which 5 were waited for; matrix products, arithmetic and copies ran while one was open for 1% of the time, Pallas kernels for 0%

commit v1 on v0

--- a/solution.py
+++ b/solution.py
@@ -155,7 +155,7 @@
     for j in range(span):
         inputs_grad = inputs_grad + short_weight[:, j][:, None, :] * dext[:, j : j + rows]
         sums.append(jnp.sum(dmixed * extended[:, span - 1 - j : span - 1 - j + rows], axis=1))
-    short_grad = lax.psum(jnp.stack(sums, axis=1), "ctx") * scale
+    short_grad = jnp.sum(lax.all_gather(jnp.stack(sums, axis=1), "ctx"), axis=0) * scale
     return (inputs_grad.astype(jnp.bfloat16), raw * scale, short_grad)
 
 

time: 1270 us -> 909 us (0.72)
  waiting for transfers between devices: 701 us -> 333 us
    psum x1 -> x0, waiting for transfers between devices: 478 us -> none  [shards(): short_grad = lax.psum(jnp.stack(sums, axis=1), 'ctx') * scale]
    all_gather x0 -> x1, waiting for transfers between devices: none -> 110 us  [shards(): lax.all_gather(jnp.stack(sums, axis=1), 'ctx')]
where the time goes in v1:
time: 909 us; the launch traced here: 898 us
  waiting for transfers between devices  333 us (37%)
  blocking collectives  217 us (24%)
  local copies, waits for them, and re-layouts  146 us (16%)
  matrix products  124 us (14%)
  other arithmetic  44.9 us (5%)
  starting transfers between devices  17.6 us (2%)
  between operations  15 us (2%)
    all_to_all x1, blocking collectives, shards(): lax.all_to_all(back, 'ctx', split_axis=3, concat_axis=2, tiled=True)  166 us
    all_to_all x1, waiting for transfers between devices, shards(): lax.all_to_all(columns, 'ctx', split_axis=2, concat_axis=3, tiled=True)  161 us
    all_gather x1, waiting for transfers between devices, shards(): lax.all_gather(jnp.stack(sums, axis=1), 'ctx')  110 us
    all_to_all x1, blocking collectives, shards(): lax.all_to_all(parted, 'ctx', split_axis=1, concat_axis=1, tiled=True)  51.2 us
    all_to_all x1, waiting for transfers between devices, shards(): lax.all_to_all(blocks, 'ctx', split_axis=1, concat_axis=1, tiled=True)  40.4 us
    dot_general x1, matrix products, section_one(): real_part = jnp.einsum('kn,bnmc->bkmc', cos_a, blocks, precision=HIGH)  23.9 us
    slice x3, local copies, waits for them, and re-layouts, section_two(): real_in, imag_in = (parts[0], parts[1])  21.6 us
    squeeze x2, local copies, waits for them, and re-layouts, section_two(): real_in, imag_in = (parts[0], parts[1])  20.6 us
  transfers between devices with their start and end apart: 6, of which 5 were waited for; matrix products, arithmetic and copies ran while one was open for 1% of the time, Pallas kernels for 0%

profile of v1, /device:TPU:0, one launch (start us, length us, event | category | flops | bytes accessed | tf_op | source)
XLA Modules:
  0.0 897.7 jit_solution(3459079894898176351)
XLA Ops:
  17.1 3.0 stack.69
  20.1 19.3 %all-gather.4.cloned.1.call-done = bf16[128,4096]{1,0:T(8,128)(2,1)} async-done(((bf16[128,2048]{1,0:T(8,128)(2,1)}), bf16[128,4096]{1,0:T(8,128)(2,1)}) %all-gather.4.cloned.1.call-update) | async-done | bytes 1048592 | tf_op jit(solution)/shard_map/all_gather | solution.py:125
  39.4 13.1 %fusion.17 = (f32[128,2048]{1,0:T(8,128)}, f32[128,2048]{1,0:T(8,128)}) fusion(f32[3,128,2048]{2,1,0:T(8,128)S(1)} %multiply_add_fusion, bf16[128,4096]{1,0:T(8,128)(2,1)} %all-gather.4.cloned.1.call-done, bf16[2048,4096]{1,0:T(8,128)(2,1)} %param.8), kind=kOutput, calls=%fused_computation.48 | convolution fusion | flops 2147745792 | bytes 20971520 | tf_op jit(solution)/shard_map/dot_general | solution.py:124
  54.3 3.2 pad_maximum_fusion.13
  57.5 3.0 copy.32
  60.5 7.9 all-to-all-start
  68.5 40.4 %all-to-all-done = f32[3,64,2,2048]{3,2,0,1:T(2,128)S(1)} async-done(((f32[3,64,2,2048]{3,2,0,1:T(2,128)}), f32[3,64,2,2048]{3,2,0,1:T(2,128)S(1)}, u32[]{:S(2)}, u32[]{:S(2)}) %all-to-all-start) | async-done | bytes 3145760 | tf_op jit(solution)/shard_map/all_to_all | solution.py:135
  108.9 11.2 %fusion.13 = f32[3,2,2048,128]{3,2,1,0:T(8,128)S(1)} fusion(f32[3,64,2,2048]{3,2,0,1:T(2,128)S(1)} %all-to-all-done), kind=kOutput, calls=%fused_computation.35 | convolution fusion | flops 1208074240 | bytes 9437184 | tf_op jit(solution)/shard_map/kn,bnmc->bkmc/dot_general | solution.py:29
  120.1 23.9 %fusion.1 = (f32[1,3,128,2,2048]{2,4,3,1,0:T(8,128)}, f32[1,3,128,2,2048]{2,4,3,1,0:T(8,128)}) fusion(f32[3,2,2048,128]{3,2,1,0:T(8,128)S(1)} %fusion.13, f32[128,2]{0,1:T(2,128)S(1)} %get-tuple-element.35, f32[128,2]{0,1:T(2,128)S(1)} %get-tuple-element.34, f32[3,64,2,2048]{3,2,0,1:T(2,128)S(1)} %all-to-all-done), kind=kOutput, calls=%fused_computation.7 | convolution fusion | flops 1219084288 | bytes 22022144 | tf_op jit(solution)/shard_map/kn,bnmc->bkmc/dot_general | solution.py:28
  144.1 9.9 %pad_maximum_fusion = f32[2,3,128,2,2048]{2,4,3,1,0:T(8,128)} fusion(f32[1,3,128,2,2048]{2,4,3,1,0:T(8,128)} %get-tuple-element.12, f32[1,3,128,2,2048]{2,4,3,1,0:T(8,128)} %get-tuple-element.11), kind=kLoop, calls=%fused_computation | loop fusion | flops 3145728 | bytes 25165824 | tf_op jit(solution)/shard_map/stack | solution.py:37
  154.0 19.3 %copy.35 = f32[2,3,128,2,2048]{4,3,1,0,2:T(2,128)} copy(f32[2,3,128,2,2048]{2,4,3,1,0:T(8,128)} %pad_maximum_fusion) | data formatting | bytes 25165824 | tf_op jit(solution)/shard_map/stack | solution.py:37
  173.4 6.8 all-to-all-start.1
  180.4 160.9 %all-to-all-done.1 = f32[2,3,128,2,2048]{4,3,1,0,2:T(2,128)} async-done(((f32[2,3,128,2,2048]{4,3,1,0,2:T(2,128)}), f32[2,3,128,2,2048]{4,3,1,0,2:T(2,128)}, u32[]{:S(2)}, u32[]{:S(2)}) %all-to-all-start.1) | async-done | bytes 12582944 | tf_op jit(solution)/shard_map/all_to_all | solution.py:139
  341.3 6.3 copy.36
  347.6 3.9 fusion.131
  351.5 8.9 copy.37
  360.4 10.3 %copy.38 = f32[3,2,128,2048]{2,3,1,0:T(8,128)} copy(f32[3,2,128,2048]{3,1,2,0:T(2,128)} %bitcast.142) | data formatting | bytes 12582912 | tf_op jit(solution)/shard_map/squeeze | solution.py:45
  370.7 9.9 %fusion.29 = f32[3,2,2048,128]{3,2,1,0:T(8,128)} fusion(f32[3,2,128,2048]{2,3,1,0:T(8,128)} %copy.38), kind=kOutput, calls=%fused_computation.70 | convolution fusion | flops 2416148480 | bytes 12582912 | tf_op jit(solution)/shard_map/qn,bknc->bkqc/dot_general | solution.py:46
  380.7 8.8 copy.39
  389.5 10.2 %copy.40 = f32[3,2,128,2048]{2,3,1,0:T(8,128)} copy(f32[3,2,128,2048]{3,1,2,0:T(2,128)} %bitcast.143) | data formatting | bytes 12582912 | tf_op jit(solution)/shard_map/squeeze | solution.py:45
  399.7 8.1 fusion.27
  407.9 7.9 add_bitcast_fusion.1
  415.9 5.4 subtract_bitcast_fusion.1
  421.3 2.6 add_bitcast_fusion.4
  423.9 3.7 subtract_bitcast_fusion.4
  427.6 8.5 fusion.4
  436.2 5.7 fusion.5
  442.0 5.7 fusion.8
  447.6 10.8 %subtract_bitcast_fusion = (f32[1,3,2,128,2048]{3,4,2,1,0:T(8,128)S(1)}, f32[1,3,2,128,2048]{3,4,2,1,0:T(8,128)}) fusion(f32[3,2,2048,128]{3,2,1,0:T(8,128)S(1)} %fusion.8, f32[2,128]{1,0:T(2,128)S(1)} %get-tuple-element.33, f32[2,128]{1,0:T(2,128)S(1)} %get-tuple-element.32, f32[3,2,2048,128]{3,2,1,0:T(8,128)S(1)} %fusion.4, ...), kind=kOutput, calls=%fused_computation.13 | convolution fusion | flops 2430304256 | bytes 31459328 | tf_op jit(solution)/shard_map/nq,bkqc->bknc/dot_general | solution.py:62
  458.4 8.1 pad_maximum_fusion.1
  466.5 19.3 %copy.43 = f32[2,3,2,128,2048]{4,2,1,0,3:T(2,128)} copy(f32[2,3,2,128,2048]{3,4,2,1,0:T(8,128)} %pad_maximum_fusion.1) | data formatting | bytes 25165824 | tf_op jit(solution)/shard_map/stack | solution.py:71
  485.9 166.0 %all_to_all.40 = f32[2,3,2,128,2048]{4,2,1,0,3:T(2,128)S(1)} all-to-all(f32[2,3,2,128,2048]{4,2,1,0,3:T(2,128)} %copy.43), channel_id=1, replica_groups=mesh['ctx'=64,'tp'=2] {'ctx'}, dimensions={3} | all-to-all | bytes 25165824 | tf_op jit(solution)/shard_map/all_to_all | solution.py:142
  651.9 2.8 copy.44
  654.7 3.9 fusion.130
  658.6 5.6 copy.45
  664.2 8.5 squeeze.33
  672.7 7.4 fusion.41
  680.1 5.6 copy.46
  685.7 8.6 squeeze.34
  694.4 6.5 multiply_bitcast_fusion
  700.9 2.4 copy.47
  703.3 51.2 %all_to_all.41 = f32[3,64,2,2048]{3,2,0,1:T(2,128)S(1)} all-to-all(f32[3,64,2,2048]{3,2,0,1:T(2,128)S(1)} %copy.47), channel_id=1, replica_groups=mesh['ctx'=64,'tp'=2] {'ctx'}, dimensions={1} | all-to-all | bytes 6291456 | tf_op jit(solution)/shard_map/all_to_all | solution.py:144
  754.5 2.4 slice_multiply_fusion.2
  756.9 3.1 squeeze.35
  760.0 2.9 squeeze.36
  769.2 3.3 multiply_reduce_fusion.2
  775.0 110.5 %all-gather.6.cloned.1.call-done = f32[192,3,2048]{2,1,0:T(4,128)} async-done(((f32[3,3,2048]{2,1,0:T(4,128)}), f32[192,3,2048]{2,1,0:T(4,128)}) %all-gather.6.cloned.1.call-update) | async-done | bytes 4718608 | tf_op jit(solution)/shard_map/all_gather | solution.py:158
  885.4 4.2 reduce_sum.39
  (90 shorter events, 21.4 us)
Async XLA Ops:
  7.2 6.6 copy-start.16
  7.2 32.2 %all-gather.4.cloned.1.call-start = ((), (), s32[]{:S(2)}) async-start(), calls=%async_computation.4 | async-start | bytes 1572864 | tf_op jit(solution)/shard_map/all_gather | solution.py:125
  8.3 5.5 collective-permute-start
  12.1 2.2 copy-start.17
  12.1 2.2 copy-start.19
  12.1 2.1 copy-start.21
  14.2 1.7 copy-start
  15.9 36.6 %copy-start.4 = (f32[3,128,2048]{2,1,0:T(8,128)}, f32[3,128,2048]{2,1,0:T(8,128)S(1)}, u32[]{:S(2)}) copy-start(f32[3,128,2048]{2,1,0:T(8,128)S(1)} %multiply_add_fusion) | copy-start | bytes 9437188
  60.5 48.4 %all-to-all-start = ((f32[3,64,2,2048]{3,2,0,1:T(2,128)}), f32[3,64,2,2048]{3,2,0,1:T(2,128)S(1)}, u32[]{:S(2)}, u32[]{:S(2)}) async-start(f32[3,64,2,2048]{3,2,0,1:T(2,128)} %copy.32), calls=%async_computation | async-start | bytes 6291456 | tf_op jit(solution)/shard_map/all_to_all | solution.py:135
  173.4 167.9 %all-to-all-start.1 = ((f32[2,3,128,2,2048]{4,3,1,0,2:T(2,128)}), f32[2,3,128,2,2048]{4,3,1,0,2:T(2,128)}, u32[]{:S(2)}, u32[]{:S(2)}) async-start(f32[2,3,128,2,2048]{4,3,1,0,2:T(2,128)} %copy.35), calls=%async_computation.1 | async-start | bytes 25165824 | tf_op jit(solution)/shard_map/all_to_all | solution.py:139
  180.2 705.2 %all-gather.6.cloned.1.call-start = ((), (), s32[]{:S(2)}) async-start(), calls=%async_computation.5 | async-start | bytes 6389760 | tf_op jit(solution)/shard_map/all_gather | solution.py:158
  360.4 20.3 %slice-start.2 = ((s8[6291456]{0:T(1024)(128)(4,1)}), s8[2097152]{0:T(1024)(128)(4,1)S(1)}, s32[]{:S(2)}) async-start(s8[6291456]{0:T(1024)(128)(4,1)} %bitcast.144), calls=%async_computation.8 | async-start | bytes 4194304
  370.7 10.0 %slice-start.3 = ((s8[6291456]{0:T(1024)(128)(4,1)}), s8[4194304]{0:T(1024)(128)(4,1)S(1)}, s32[]{:S(2)}) async-start(s8[6291456]{0:T(1024)(128)(4,1)} %bitcast.144), calls=%async_computation.9 | async-start | bytes 8388608
  399.7 8.1 copy-start.2
  399.7 16.1 %slice-start = ((s8[6291456]{0:T(1024)(128)(4,1)}), s8[4194304]{0:T(1024)(128)(4,1)S(1)}, s32[]{:S(2)}) async-start(s8[6291456]{0:T(1024)(128)(4,1)} %bitcast.138), calls=%async_computation.6 | async-start | bytes 8388608
  407.9 8.0 slice-start.1
  427.6 8.5 copy-start.9
  427.6 8.5 copy-start.10
  427.6 8.5 copy-start.11
  436.2 5.7 copy-start.6
  436.2 5.7 copy-start.7
  436.2 5.7 copy-start.8
  672.7 7.4 copy-start.3
  685.7 8.6 copy-start.12
  756.9 6.0 copy-start.5
  762.9 1.6 copy-start.13
  762.9 1.9 copy-start.14
  765.3 3.9 copy-start.1
  765.3 3.9 copy-start.18
  765.3 3.9 copy-start.20
  765.3 3.9 copy-start.22
  765.3 3.4 collective-permute-start.1
  769.2 4.1 copy-start.15
Sparse Core Ops, SparseCore 0:
  9.7 29.6 all-gather.3
  773.4 112.0 all-gather.5
